TPU v7x, 32 devices: a whole 2x2x4 slice. The times are simulated.
32 devices in a mesh: group: 2 (over x), ctx: 16 (over z, y, core).
Axes of the slice: x: 2, y: 2, z: 4, core: 2. Of those that a mesh axis runs over, the one named last changes fastest.
Arguments:
- normed_hidden: bfloat16 [4096, 8192], P(('group', 'ctx')), parts along dimension 0, may hold values from -6 to 6
- queries: bfloat16 [4096, 4096], P(('group', 'ctx')), parts along dimension 0, may hold values from -45 to 45
- keys: bfloat16 [4096, 512], P(('group', 'ctx')), parts along dimension 0, may hold values from -6 to 6
- value_frozen_matrix: bfloat16 [8192, 512], P('ctx'), may hold values from -0.0625 to 0.0625
- adapter_down_weight: bfloat16 [8192, 64], replicated, may hold values from -0.0625 to 0.0625
- adapter_up_weight: bfloat16 [64, 512], replicated, may hold values from -0.75 to 0.75
- block_slot_index: int32 [64], P(('group', 'ctx')), parts along dimension 0, may hold values from 0 to 31, each once
Outputs:
- attended: bfloat16 [4096, 4096], P(('group', 'ctx')), parts along dimension 0
There are 2 independent parts, one for each index of `group`. A program takes and returns all parts, laid end to end along the dimension named above; an argument that names none is the same for every part. Nothing has to cross between parts.
Inputs may be any that keep to these rules, and one draw needn't show every extreme that they name: `block_slot_index`: each of the 32 blocks is named once; slot j holds rows j*64 to (j+1)*64 - 1.
All inputs are finite; a program needn't handle non-finite values.
Results may differ from a plain program's by a relative error of at most 0.0054.
Values may be sent and summed in bfloat16 or wider, within the bound.
No kernel may reach another device: no remote copies, remote signals or barrier semaphores. Data moves between devices by JAX's collectives and lax.ppermute only.
A program may use at most 192 MiB of HBM per device.

v0:
```python
import jax
import jax.numpy as jnp
from jax import lax
from jax.sharding import PartitionSpec as P

QH = 32
KVH = 4
HD = 128
BLK = 64


def shards(
    normed_hidden,
    queries,
    keys,
    value_frozen_matrix,
    adapter_down_weight,
    adapter_up_weight,
    block_slot_index,
):
    tokens = normed_hidden.shape[0]
    scale = 1.0 / HD**0.5
    offsets = jnp.arange(BLK, dtype=jnp.int32)
    table = lax.all_gather(block_slot_index, "ctx", axis=0, tiled=True)
    my_pos = (block_slot_index[:, None] * BLK + offsets[None, :]).reshape(tokens)
    frozen_output = jnp.dot(
        normed_hidden,
        lax.all_gather(value_frozen_matrix, "ctx", axis=0, tiled=True),
        preferred_element_type=jnp.float32,
    )
    low_rank_output = jnp.dot(
        normed_hidden, adapter_down_weight, preferred_element_type=jnp.float32
    ).astype(jnp.bfloat16)
    value_output = (
        frozen_output
        + 0.5 * jnp.dot(low_rank_output, adapter_up_weight, preferred_element_type=jnp.float32)
    ).astype(jnp.bfloat16)
    slots_here = tokens // BLK
    query_slots = [
        queries[which * BLK : (which + 1) * BLK].reshape(BLK, KVH, QH // KVH, HD)
        for which in range(slots_here)
    ]
    pos_slots = [my_pos[which * BLK : (which + 1) * BLK] for which in range(slots_here)]
    shape_stat = (KVH, QH // KVH, BLK)
    init = tuple(
        (
            (
                jnp.full(shape_stat, -1e30, jnp.float32),
                jnp.zeros(shape_stat, jnp.float32),
                jnp.zeros(shape_stat + (HD,), jnp.float32),
            )
            for which in range(slots_here)
        )
    )
    key_piece = lax.all_gather(keys, "ctx", axis=0, tiled=True)
    count = key_piece.shape[0]
    key_pos = (table[:, None] * BLK + offsets[None, :]).reshape(count)
    key_three = key_piece.reshape(count, KVH, HD)
    value_three = lax.all_gather(value_output, "ctx", axis=0, tiled=True).reshape(count, KVH, HD)
    lowest_key = jnp.min(key_pos)
    updated = []
    for attend_which in range(slots_here):
        q_part = query_slots[attend_which]
        q_pos = pos_slots[attend_which]

        def update(state, q_part=q_part, q_pos=q_pos):
            top, total, accum = state
            scores = (
                jnp.einsum("tkgd,skd->kgts", q_part, key_three, preferred_element_type=jnp.float32)
                * scale
            )
            visible = (q_pos[:, None] >= key_pos[None, :])[None, None]
            scores = jnp.where(visible, scores, -1e30)
            top_new = jnp.maximum(top, jnp.max(scores, axis=-1))
            weights = jnp.where(visible, jnp.exp(scores - top_new[..., None]), 0.0)
            total = jnp.sum(weights, axis=-1)
            accum = jnp.einsum(
                "kgts,skd->kgtd",
                weights.astype(jnp.bfloat16),
                value_three,
                preferred_element_type=jnp.float32,
            )
            return (top_new, total, accum)

        def keep(state):
            return state

        updated.append(lax.cond(lowest_key <= jnp.max(q_pos), update, keep, init[attend_which]))
    states = tuple(updated)
    outputs = []
    for which in range(slots_here):
        result = states[which][2] / states[which][1][..., None]
        outputs.append(
            jnp.transpose(result, (2, 0, 1, 3)).reshape(BLK, QH * HD).astype(jnp.bfloat16)
        )
    return jnp.concatenate(outputs, axis=0)


def solution(mesh):
    in_specs = (
        P(("group", "ctx"), None),
        P(("group", "ctx"), None),
        P(("group", "ctx"), None),
        P("ctx", None),
        P(),
        P(),
        P(("group", "ctx")),
    )
    out_specs = P(("group", "ctx"), None)
    return jax.shard_map(shards, mesh=mesh, in_specs=in_specs, out_specs=out_specs, check_vma=False)
```

profile of v0, /device:TPU:0, one launch (start us, length us, event | category | flops | bytes accessed | tf_op | source)
XLA Modules:
  0.0 216.8 jit_solution(570349210918793714)
XLA Ops:
  6.5 0.0 copy-start
  6.5 0.0 copy-start.6
  6.5 0.0 copy-start.3
  6.5 0.0 copy-start.4
  6.5 0.0 copy-start.5
  6.5 0.0 all-gather.6.cloned.1.call-start
  6.6 0.7 all-gather.6.cloned.1.call-update
  7.3 0.0 all-gather.8.cloned.1.call-start
  7.3 79.2 %all-gather.6.cloned.1.call-done = bf16[8192,512]{1,0:T(8,128)(2,1)} async-done(((bf16[512,512]{1,0:T(8,128)(2,1)}), bf16[8192,512]{1,0:T(8,128)(2,1)}) %all-gather.6.cloned.1.call-update) | async-done | bytes 8388624 | tf_op jit(solution)/shard_map/all_gather | solution.py:28
  86.6 0.0 copy-done
  86.6 4.6 %fusion.31 = f32[128,512]{1,0:T(8,128)S(1)} fusion(bf16[128,8192]{1,0:T(8,128)(2,1)S(1)} %copy-done, bf16[8192,512]{1,0:T(8,128)(2,1)} %all-gather.6.cloned.1.call-done), kind=kOutput, calls=%fused_computation.52 | convolution fusion | flops 1073741824 | bytes 10747904 | tf_op jit(solution)/shard_map/dot_general | solution.py:26
  91.2 0.0 copy-done.3
  91.2 2.4 %fusion.27 = bf16[128,512]{1,0:T(8,128)(2,1)} fusion(f32[128,512]{1,0:T(8,128)S(1)} %fusion.31, bf16[64,512]{1,0:T(8,128)(2,1)} %param.16, bf16[128,8192]{1,0:T(8,128)(2,1)S(1)} %copy-done, bf16[8192,64]{0,1:T(8,128)(2,1)S(1)} %copy-done.3), kind=kOutput, calls=%fused_computation.36 | convolution fusion | flops 142811136 | bytes 3604480 | tf_op jit(solution)/shard_map/dot_general | solution.py:36
  93.6 0.0 all-gather.8.cloned.1.call-update
  93.6 0.0 all-gather.4.cloned.1.call-start
  93.7 0.0 copy-done.4
  93.7 0.8 copy.14
  94.4 0.0 all-gather.4.cloned.1.call-update
  94.5 0.0 copy-done.6
  94.5 0.6 dynamic-slice
  95.6 0.0 copy-done.5
  95.6 0.2 dynamic-update-slice
  95.9 9.9 %all-reduce = s32[32]{0:T(128)S(1)} all-reduce(s32[32]{0:T(128)S(1)} %dynamic-update-slice), channel_id=1, replica_groups=mesh['group'=2,'ctx'=16] {'ctx'}, use_global_device_ids=true, to_apply=%add | all-reduce | flops 32 | bytes 256
  105.8 0.1 iota_add_fusion.1
  105.9 0.7 slice_reduce_fusion.1
  106.6 0.7 iota_add_fusion
  109.7 24.1 %all-gather.8.cloned.1.call-done = bf16[2048,512]{1,0:T(8,128)(2,1)} async-done(((bf16[128,512]{1,0:T(8,128)(2,1)}), bf16[2048,512]{1,0:T(8,128)(2,1)}) %all-gather.8.cloned.1.call-update) | async-done | bytes 2097168 | tf_op jit(solution)/shard_map/all_gather | solution.py:59
  133.7 4.0 %reshape.101 = bf16[2048,4,128]{2,1,0:T(4,128)(2,1)} reshape(bf16[2048,512]{1,0:T(8,128)(2,1)} %all-gather.8.cloned.1.call-done) | data formatting | bytes 4194304 | tf_op jit(solution)/shard_map/reshape | solution.py:59
  137.7 38.0 %all-gather.4.cloned.1.call-done = bf16[2048,512]{0,1:T(8,128)(2,1)} async-done(((bf16[128,512]{0,1:T(8,128)(2,1)}), bf16[2048,512]{0,1:T(8,128)(2,1)}) %all-gather.4.cloned.1.call-update) | async-done | bytes 2097168 | tf_op jit(solution)/shard_map/all_gather | solution.py:55
  175.7 14.9 %conditional.2 = (f32[4,8,64]{2,1,0:T(8,128)S(1)}, f32[4,8,64,128]{3,2,1,0:T(8,128)S(1)}) conditional(s32[]{:T(128)} %convert_element_type.36, () %tuple.21, (s32[1,64]{1,0:T(1,128)S(1)}, s32[32,64]{1,0:T(8,128)S(1)}, bf16[128,4096]{1,0:T(8,128)(2,1)}, bf16[2048,4,128]{0,2,1:T(8,128)(2,1)}, bf16[2048,4,128]{2,1,0:T(4,128)(2,1)}) %tuple.46), branch_computations={%region_2.0_spmd, %region_3.6_spmd} | conditional | flops 2202138624 | bytes 67182896 | solution.py:88
  175.7 0.1 ge.34
  175.8 0.0 copy-start.1
  175.8 0.1 broadcast_compare_fusion
  175.9 1.2 slice_bitcast_fusion
  177.1 0.1 copy.33
  177.2 4.4 %fusion = (f32[4,8,64]{2,1,0:T(8,128)S(1)}, f32[4,2048,64,8]{1,2,3,0:T(8,128)S(1)}) fusion(pred[64,2048]{1,0:T(8,128)(4,1)S(1)} %broadcast_compare_fusion, bf16[64,4,8,128]{3,2,1,0:T(8,128)(2,1)S(1)} %bitcast.69, bf16[2048,4,128]{0,2,1:T(8,128)(2,1)} %get-tuple-element.62), kind=kOutput, calls=%fused_computation.2 | convolution fusion | flops 1086322688 | bytes 19537920 | tf_op jit(solution)/shard_map/cond/branch_1_fun/tkgd,skd->kgts/dot_general | solution.py:69
  181.7 0.0 copy-done.1
  181.7 3.8 %fusion.3 = f32[4,8,64,128]{3,2,1,0:T(8,128)S(1)} fusion(f32[4,2048,64,8]{1,2,3,0:T(8,128)S(1)} %get-tuple-element.72, f32[4,8,64]{2,1,0:T(8,128)S(1)} %broadcast_maximum_fusion, pred[64,2048]{1,0:T(8,128)(4,1)S(1)} %broadcast_compare_fusion, bf16[2048,4,128,1]{2,1,0,3:T(4,128)(2,1)S(1)} %bitcast.71), kind=kOutput, calls=%fused_computation.5 | convolution fusion | flops 1094713344 | bytes 20062208 | tf_op jit(solution)/shard_map/cond/branch_1_fun/kgts,skd->kgtd/dot_general | solution.py:77
  185.5 5.1 %fusion.2 = f32[4,8,64]{2,1,0:T(8,128)S(1)} fusion(f32[4,2048,64,8]{1,2,3,0:T(8,128)S(1)} %get-tuple-element.72, f32[4,8,64]{2,1,0:T(8,128)S(1)} %broadcast_maximum_fusion, pred[64,2048]{1,0:T(8,128)(4,1)S(1)} %broadcast_compare_fusion), kind=kLoop, calls=%fused_computation.4 | loop fusion | flops 20969472 | bytes 16924672 | tf_op jit(solution)/shard_map/cond/branch_1_fun/reduce_sum | solution.py:76
  190.6 0.3 fusion.28
  191.0 1.1 copy.17
  192.1 14.9 %conditional.3 = (f32[4,8,64]{2,1,0:T(8,128)S(1)}, f32[4,8,64,128]{3,2,1,0:T(8,128)S(1)}) conditional(s32[]{:T(128)} %convert_element_type.42, () %tuple.23, (s32[1,64]{1,0:T(1,128)S(1)}, s32[32,64]{1,0:T(8,128)S(1)}, bf16[128,4096]{1,0:T(8,128)(2,1)}, bf16[2048,4,128]{0,2,1:T(8,128)(2,1)}, bf16[2048,4,128]{2,1,0:T(4,128)(2,1)}) %tuple.47), branch_computations={%region_7.8_spmd, %region_8.11_spmd} | conditional | flops 2202138624 | bytes 67182896 | solution.py:88
  192.1 0.1 ge.39
  192.2 0.0 copy-start.2
  192.2 0.1 broadcast_compare_fusion.1
  192.3 1.2 slice_bitcast_fusion.1
  193.6 0.1 copy.34
  193.6 4.4 %fusion.13 = (f32[4,8,64]{2,1,0:T(8,128)S(1)}, f32[4,2048,64,8]{1,2,3,0:T(8,128)S(1)}) fusion(pred[64,2048]{1,0:T(8,128)(4,1)S(1)} %broadcast_compare_fusion.1, bf16[64,4,8,128]{3,2,1,0:T(8,128)(2,1)S(1)} %bitcast.70, bf16[2048,4,128]{0,2,1:T(8,128)(2,1)} %get-tuple-element.67), kind=kOutput, calls=%fused_computation.19 | convolution fusion | flops 1086322688 | bytes 19537920 | tf_op jit(solution)/shard_map/cond/branch_1_fun/tkgd,skd->kgts/dot_general | solution.py:69
  198.1 0.0 copy-done.2
  198.1 3.8 %fusion.16 = f32[4,8,64,128]{3,2,1,0:T(8,128)S(1)} fusion(f32[4,2048,64,8]{1,2,3,0:T(8,128)S(1)} %get-tuple-element.74, f32[4,8,64]{2,1,0:T(8,128)S(1)} %broadcast_maximum_fusion.1, pred[64,2048]{1,0:T(8,128)(4,1)S(1)} %broadcast_compare_fusion.1, bf16[2048,4,128,1]{2,1,0,3:T(4,128)(2,1)S(1)} %bitcast.72), kind=kOutput, calls=%fused_computation.22 | convolution fusion | flops 1094713344 | bytes 20062208 | tf_op jit(solution)/shard_map/cond/branch_1_fun/kgts,skd->kgtd/dot_general | solution.py:77
  202.0 5.1 %fusion.15 = f32[4,8,64]{2,1,0:T(8,128)S(1)} fusion(f32[4,2048,64,8]{1,2,3,0:T(8,128)S(1)} %get-tuple-element.74, f32[4,8,64]{2,1,0:T(8,128)S(1)} %broadcast_maximum_fusion.1, pred[64,2048]{1,0:T(8,128)(4,1)S(1)} %broadcast_compare_fusion.1), kind=kLoop, calls=%fused_computation.21 | loop fusion | flops 20969472 | bytes 16924672 | tf_op jit(solution)/shard_map/cond/branch_1_fun/reduce_sum | solution.py:76
  207.1 0.3 fusion.29
  207.4 0.3 copy.20
  207.8 1.4 copy_bitcast_fusion
  209.2 1.1 pad_maximum_fusion
  (5 shorter events, 0.0 us)
Async XLA Ops:
  6.5 80.0 %copy-start = (bf16[128,8192]{1,0:T(8,128)(2,1)S(1)}, bf16[128,8192]{1,0:T(8,128)(2,1)}, u32[]{:S(2)}) copy-start(bf16[128,8192]{1,0:T(8,128)(2,1)} %param.11) | copy-start | bytes 6291460
  6.5 87.9 %copy-start.6 = (u32[32]{0:T(128)S(1)}, u32[32]{0:T(128)}, u32[]{:S(2)}) copy-start(u32[32]{0:T(128)} %constant.9) | copy-start | bytes 388
  6.5 84.7 %copy-start.3 = (bf16[8192,64]{0,1:T(8,128)(2,1)S(1)}, bf16[8192,64]{0,1:T(8,128)(2,1)}, u32[]{:S(2)}) copy-start(bf16[8192,64]{0,1:T(8,128)(2,1)} %param.15) | copy-start | bytes 3145732
  6.5 87.1 %copy-start.4 = (bf16[128,512]{1,0:T(8,128)(2,1)S(1)}, bf16[128,512]{1,0:T(8,128)(2,1)}, u32[]{:S(2)}) copy-start(bf16[128,512]{1,0:T(8,128)(2,1)} %param.13) | copy-start | bytes 393220
  6.5 89.1 %copy-start.5 = (s32[2]{0:T(128)S(1)}, s32[2]{0:T(128)}, u32[]{:S(2)}) copy-start(s32[2]{0:T(128)} %param.17) | copy-start | bytes 28
  6.5 80.0 %all-gather.6.cloned.1.call-start = ((), (), s32[]{:S(2)}) async-start(), calls=%async_computation.1 | async-start | bytes 8912896 | tf_op jit(solution)/shard_map/all_gather | solution.py:28
  7.3 126.5 %all-gather.8.cloned.1.call-start = ((), (), s32[]{:S(2)}) async-start(), calls=%async_computation.2 | async-start | bytes 2228224 | tf_op jit(solution)/shard_map/all_gather | solution.py:59
  93.6 82.1 %all-gather.4.cloned.1.call-start = ((), (), s32[]{:S(2)}) async-start(), calls=%async_computation | async-start | bytes 2228224 | tf_op jit(solution)/shard_map/all_gather | solution.py:55
  175.8 5.9 %copy-start.1 = (bf16[2048,4,128]{2,1,0:T(4,128)(2,1)S(1)}, bf16[2048,4,128]{2,1,0:T(4,128)(2,1)}, u32[]{:S(2)}) copy-start(bf16[2048,4,128]{2,1,0:T(4,128)(2,1)} %get-tuple-element.63) | copy-start | bytes 6291460 | tf_op jit(solution)/shard_map/cond
  192.2 5.9 %copy-start.2 = (bf16[2048,4,128]{2,1,0:T(4,128)(2,1)S(1)}, bf16[2048,4,128]{2,1,0:T(4,128)(2,1)}, u32[]{:S(2)}) copy-start(bf16[2048,4,128]{2,1,0:T(4,128)(2,1)} %get-tuple-element.68) | copy-start | bytes 6291460 | tf_op jit(solution)/shard_map/cond
Sparse Core Ops, SparseCore 0:
  9.5 77.0 all-gather.5
  93.7 39.9 all-gather.7
  135.9 39.7 all-gather.3
where the time goes:
time: 217 us
  waiting for transfers between devices  142 us (65%)
  matrix products  23.5 us (11%)
  between operations  16.1 us (7%)
  other arithmetic  13.7 us (6%)
  local copies, waits for them, and re-layouts  11.2 us (5%)
  blocking collectives  9.93 us (5%)
    all_gather x1, waiting for transfers between devices, shards(): lax.all_gather(value_frozen_matrix, 'ctx', axis=0, tiled=True)  79.2 us
    all_gather x1, waiting for transfers between devices, shards(): key_piece = lax.all_gather(keys, 'ctx', axis=0, tiled=True)  38 us
    all_gather x1, waiting for transfers between devices, shards(): lax.all_gather(value_output, 'ctx', axis=0, tiled=True)  24.1 us
    reduce_sum x2, other arithmetic, update(): total = jnp.sum(weights, axis=-1)  10.2 us
    unnamed x1, blocking collectives  9.93 us
    dot_general x2, matrix products, update(): jnp.einsum('tkgd,skd->kgts', q_part, key_three, preferred_element_type=jn...  8.88 us
    dot_general x2, matrix products, update(): jnp.einsum('kgts,skd->kgtd', weights.astype(jnp.bfloat16), value_three, p...  7.67 us
    dot_general x1, matrix products, shards(): jnp.dot(normed_hidden, lax.all_gather(value_frozen_matrix, 'ctx', axis=0,...  4.63 us
  transfers between devices with their start and end apart: 3, of which 3 were waited for; matrix products, arithmetic and copies ran while one was open for 3% of the time, Pallas kernels for 0%

commit v1 on v0

--- a/solution.py
+++ b/solution.py
@@ -7,6 +7,25 @@
 KVH = 4
 HD = 128
 BLK = 64
+
+
+def collect(array, axis, dim):
+    size, here, rows = (lax.axis_size(axis), lax.axis_index(axis), array.shape[dim])
+    right = [(i, (i + 1) % size) for i in range(size)]
+    downward = [(i, (i - 1) % size) for i in range(size)]
+    out = jnp.zeros((*array.shape[:dim], size * rows, *array.shape[dim + 1 :]), array.dtype)
+    out = lax.dynamic_update_slice_in_dim(out, array, here * rows, axis=dim)
+    from_left = from_right = array
+    half = size // 2
+    for turn in range(1, half + 1):
+        from_left = lax.ppermute(from_left, axis, right)
+        out = lax.dynamic_update_slice_in_dim(out, from_left, (here - turn) % size * rows, axis=dim)
+        if turn < size - half:
+            from_right = lax.ppermute(from_right, axis, downward)
+            out = lax.dynamic_update_slice_in_dim(
+                out, from_right, (here + turn) % size * rows, axis=dim
+            )
+    return out
 
 
 def shards(
@@ -24,9 +43,7 @@
     table = lax.all_gather(block_slot_index, "ctx", axis=0, tiled=True)
     my_pos = (block_slot_index[:, None] * BLK + offsets[None, :]).reshape(tokens)
     frozen_output = jnp.dot(
-        normed_hidden,
-        lax.all_gather(value_frozen_matrix, "ctx", axis=0, tiled=True),
-        preferred_element_type=jnp.float32,
+        normed_hidden, collect(value_frozen_matrix, "ctx", 0), preferred_element_type=jnp.float32
     )
     low_rank_output = jnp.dot(
         normed_hidden, adapter_down_weight, preferred_element_type=jnp.float32

time: 217 us -> 209 us (0.963)
  waiting for transfers between devices: 142 us -> 53.5 us
  starting transfers between devices: 0.12 us -> 52.3 us
  local copies, waits for them, and re-layouts: 11.2 us -> 33.5 us
  blocking collectives: 9.93 us -> 14.2 us
    all_gather x1 -> x0, waiting for transfers between devices: 79.2 us -> none  [shards(): lax.all_gather(value_frozen_matrix, 'ctx', axis=0, tiled=True)]
    ppermute x0 -> x15, starting transfers between devices: none -> 52.3 us  [the longest x8 42.1 us: collect(): from_left = lax.ppermute(from_left, axis, right)]
    all_gather x1, waiting for transfers between devices: 38 us -> 0.02 us  [shards(): key_piece = lax.all_gather(keys, 'ctx', axis=0, tiled=True)]
    ppermute x0 -> x15, waiting for transfers between devices: none -> 28.1 us  [the longest x8 28.1 us: collect(): from_left = lax.ppermute(from_left, axis, right)]
    dynamic_update_slice x0 -> x16, local copies, waits for them, and re-layouts: none -> 23.8 us  [the longest x8 11.9 us: collect(): lax.dynamic_update_slice_in_dim(out, from_left, (here - turn) % size * ro...]
    unnamed x1, blocking collectives: 9.93 us -> 14.2 us
    reshape x1 -> x0, local copies, waits for them, and re-layouts: 3.96 us -> none  [shards(): lax.all_gather(value_output, 'ctx', axis=0, tiled=True)]
    broadcast_in_dim x0 -> x1, local copies, waits for them, and re-layouts: none -> 3.76 us  [collect(): jnp.zeros((*array.shape[:dim], size * rows, *array.shape[dim + 1:]), arra...]
  transfers between devices with their start and end apart: 3 -> 17, of which waited for: 3 -> 6; matrix products, arithmetic and copies ran while one was open for 3% -> 19% of each run, Pallas kernels for 0% -> 0%
where the time goes in v1:
time: 209 us
  waiting for transfers between devices  53.5 us (26%)
  starting transfers between devices  52.3 us (25%)
  local copies, waits for them, and re-layouts  33.5 us (16%)
  matrix products  24.9 us (12%)
  between operations  16.5 us (8%)
  blocking collectives  14.2 us (7%)
  other arithmetic  13.6 us (7%)
    ppermute x8, starting transfers between devices, collect(): from_left = lax.ppermute(from_left, axis, right)  42.1 us
    ppermute x8, waiting for transfers between devices, collect(): from_left = lax.ppermute(from_left, axis, right)  28.1 us
    all_gather x1, waiting for transfers between devices, shards(): lax.all_gather(value_output, 'ctx', axis=0, tiled=True)  25.4 us
    unnamed x1, blocking collectives  14.2 us
    dynamic_update_slice x8, local copies, waits for them, and re-layouts, collect(): lax.dynamic_update_slice_in_dim(out, from_left, (here - turn) % size * ro...  11.9 us
    dynamic_update_slice x7, local copies, waits for them, and re-layouts, collect(): lax.dynamic_update_slice_in_dim(out, from_right, (here + turn) % size * r...  11.1 us
    ppermute x7, starting transfers between devices, collect(): from_right = lax.ppermute(from_right, axis, downward)  10.2 us
    reduce_sum x2, other arithmetic, update(): total = jnp.sum(weights, axis=-1)  10.1 us
  transfers between devices with their start and end apart: 17, of which 6 were waited for; matrix products, arithmetic and copies ran while one was open for 19% of the time, Pallas kernels for 0%

profile of v1, /device:TPU:0, one launch (start us, length us, event | category | flops | bytes accessed | tf_op | source)
XLA Modules:
  0.0 208.7 jit_solution(11177010414360955388)
XLA Ops:
  6.5 0.5 collective-permute-start
  7.0 5.0 %collective-permute-start.1 = (bf16[512,512]{1,0:T(8,128)(2,1)}, bf16[512,512]{1,0:T(8,128)(2,1)}, u32[]{:S(2)}, u32[]{:S(2)}) collective-permute-start(bf16[512,512]{1,0:T(8,128)(2,1)} %param.14), channel_id=1, source_target_pairs={{0,15},{1,0},{2,1},{3,2},{4,3},{5,4},{6,5},{7,6},{8,7},{9,8},{10,9... | collective-permute-start | bytes 1572872 | tf_op jit(solution)/shard_map/ppermute | solution.py:24
  12.1 7.2 %collective-permute-done = bf16[512,512]{1,0:T(8,128)(2,1)} collective-permute-done((bf16[512,512]{1,0:T(8,128)(2,1)}, bf16[512,512]{1,0:T(8,128)(2,1)}, u32[]{:S(2)}, u32[]{:S(2)}) %collective-permute-start) | collective-permute-done | bytes 524320 | tf_op jit(solution)/shard_map/ppermute | solution.py:21
  19.3 2.4 %collective-permute-start.2 = (bf16[512,512]{1,0:T(8,128)(2,1)}, bf16[512,512]{1,0:T(8,128)(2,1)}, u32[]{:S(2)}, u32[]{:S(2)}) collective-permute-start(bf16[512,512]{1,0:T(8,128)(2,1)} %collective-permute-done), channel_id=1, source_target_pairs={{0,1},{1,2},{2,3},{3,4},{4,5},{5,6},{6,7},{7,8},{8,9},{9,10},{10,1... | collective-permute-start | bytes 1572872 | tf_op jit(solution)/shard_map/ppermute | solution.py:21
  21.7 2.1 collective-permute-start.3
  23.8 7.2 %collective-permute-done.2 = bf16[512,512]{1,0:T(8,128)(2,1)} collective-permute-done((bf16[512,512]{1,0:T(8,128)(2,1)}, bf16[512,512]{1,0:T(8,128)(2,1)}, u32[]{:S(2)}, u32[]{:S(2)}) %collective-permute-start.2) | collective-permute-done | bytes 524320 | tf_op jit(solution)/shard_map/ppermute | solution.py:21
  31.0 4.4 %collective-permute-start.4 = (bf16[512,512]{1,0:T(8,128)(2,1)}, bf16[512,512]{1,0:T(8,128)(2,1)S(1)}, u32[]{:S(2)}, u32[]{:S(2)}) collective-permute-start(bf16[512,512]{1,0:T(8,128)(2,1)} %collective-permute-done.2), channel_id=1, source_target_pairs={{0,1},{1,2},{2,3},{3,4},{4,5},{5,6},{6,7},{7,8},{8,9},{9,10},{10,1... | collective-permute-start | bytes 1572872 | tf_op jit(solution)/shard_map/ppermute | solution.py:21
  35.5 7.1 %collective-permute-done.4 = bf16[512,512]{1,0:T(8,128)(2,1)S(1)} collective-permute-done((bf16[512,512]{1,0:T(8,128)(2,1)}, bf16[512,512]{1,0:T(8,128)(2,1)S(1)}, u32[]{:S(2)}, u32[]{:S(2)}) %collective-permute-start.4) | collective-permute-done | bytes 524320 | tf_op jit(solution)/shard_map/ppermute | solution.py:21
  42.7 6.6 %collective-permute-start.6 = (bf16[512,512]{1,0:T(8,128)(2,1)S(1)}, bf16[512,512]{1,0:T(8,128)(2,1)}, u32[]{:S(2)}, u32[]{:S(2)}) collective-permute-start(bf16[512,512]{1,0:T(8,128)(2,1)S(1)} %collective-permute-done.4), channel_id=1, source_target_pairs={{0,1},{1,2},{2,3},{3,4},{4,5},{5,6},{6,7},{7,8},{8,9},{9,10},{10,1... | collective-permute-start | bytes 1572872 | tf_op jit(solution)/shard_map/ppermute | solution.py:21
  49.3 1.7 copy.15
  51.0 0.1 collective-permute-start.7
  51.1 3.0 %collective-permute-done.6 = bf16[512,512]{1,0:T(8,128)(2,1)} collective-permute-done((bf16[512,512]{1,0:T(8,128)(2,1)S(1)}, bf16[512,512]{1,0:T(8,128)(2,1)}, u32[]{:S(2)}, u32[]{:S(2)}) %collective-permute-start.6) | collective-permute-done | bytes 524320 | tf_op jit(solution)/shard_map/ppermute | solution.py:21
  54.1 10.7 %collective-permute-start.8 = (bf16[512,512]{1,0:T(8,128)(2,1)}, bf16[512,512]{1,0:T(8,128)(2,1)}, u32[]{:S(2)}, u32[]{:S(2)}) collective-permute-start(bf16[512,512]{1,0:T(8,128)(2,1)} %collective-permute-done.6), channel_id=1, source_target_pairs={{0,1},{1,2},{2,3},{3,4},{4,5},{5,6},{6,7},{7,8},{8,9},{9,10},{10,1... | collective-permute-start | bytes 1572872 | tf_op jit(solution)/shard_map/ppermute | solution.py:21
  64.8 2.1 %convolution_multiply_fusion = f32[128,512]{0,1:T(8,128)S(1)} fusion(bf16[64,512]{1,0:T(8,128)(2,1)} %param.16, bf16[128,8192]{1,0:T(8,128)(2,1)S(1)} %copy-done, bf16[8192,64]{0,1:T(8,128)(2,1)} %param.15), kind=kOutput, calls=%fused_computation.34 | convolution fusion | flops 142680064 | bytes 3473408 | tf_op jit(solution)/shard_map/dot_general | solution.py:53
  67.0 11.8 %collective-permute-start.10 = (bf16[512,512]{1,0:T(8,128)(2,1)}, bf16[512,512]{1,0:T(8,128)(2,1)}, u32[]{:S(2)}, u32[]{:S(2)}) collective-permute-start(bf16[512,512]{1,0:T(8,128)(2,1)} %collective-permute-done.8), channel_id=1, source_target_pairs={{0,1},{1,2},{2,3},{3,4},{4,5},{5,6},{6,7},{7,8},{8,9},{9,10},{10,1... | collective-permute-start | bytes 1572872 | tf_op jit(solution)/shard_map/ppermute | solution.py:21
  78.8 3.8 %broadcast_in_dim.47 = bf16[8192,512]{1,0:T(8,128)(2,1)} broadcast(bf16[]{:T(256)} %constant.121.clone.1), dimensions={} | broadcast | bytes 8388610 | tf_op jit(solution)/shard_map/broadcast_in_dim | solution.py:16
  82.6 0.8 constant_dynamic-update-slice_fusion.15
  83.4 1.9 constant_dynamic-update-slice_fusion.14
  85.3 1.9 constant_dynamic-update-slice_fusion.13
  87.2 1.9 constant_dynamic-update-slice_fusion.12
  89.0 1.9 constant_dynamic-update-slice_fusion.11
  91.0 3.0 %collective-permute-start.12 = (bf16[512,512]{1,0:T(8,128)(2,1)}, bf16[512,512]{1,0:T(8,128)(2,1)S(1)}, u32[]{:S(2)}, u32[]{:S(2)}) collective-permute-start(bf16[512,512]{1,0:T(8,128)(2,1)} %collective-permute-done.10), channel_id=1, source_target_pairs={{0,1},{1,2},{2,3},{3,4},{4,5},{5,6},{6,7},{7,8},{8,9},{9,10},{10,1... | collective-permute-start | bytes 1572872 | tf_op jit(solution)/shard_map/ppermute | solution.py:21
  94.0 0.8 constant_dynamic-update-slice_fusion.10
  94.8 1.9 constant_dynamic-update-slice_fusion.9
  96.7 1.9 constant_dynamic-update-slice_fusion.8
  98.5 1.9 constant_dynamic-update-slice_fusion.7
  100.4 3.0 %collective-permute-start.13 = (bf16[512,512]{1,0:T(8,128)(2,1)S(1)}, bf16[512,512]{1,0:T(8,128)(2,1)S(1)}, u32[]{:S(2)}, u32[]{:S(2)}) collective-permute-start(bf16[512,512]{1,0:T(8,128)(2,1)S(1)} %collective-permute-done.11), channel_id=1, source_target_pairs={{0,15},{1,0},{2,1},{3,2},{4,3},{5,4},{6,5},{7,6},{8,7},{9,8},{10,9... | collective-permute-start | bytes 1572872 | tf_op jit(solution)/shard_map/ppermute | solution.py:24
  103.4 1.9 constant_dynamic-update-slice_fusion.6
  105.3 2.6 %collective-permute-start.14 = (bf16[512,512]{1,0:T(8,128)(2,1)S(1)}, bf16[512,512]{1,0:T(8,128)(2,1)S(1)}, u32[]{:S(2)}, u32[]{:S(2)}) collective-permute-start(bf16[512,512]{1,0:T(8,128)(2,1)S(1)} %collective-permute-done.12), channel_id=1, source_target_pairs={{0,1},{1,2},{2,3},{3,4},{4,5},{5,6},{6,7},{7,8},{8,9},{9,10},{10,1... | collective-permute-start | bytes 1572872 | tf_op jit(solution)/shard_map/ppermute | solution.py:21
  107.9 1.9 constant_dynamic-update-slice_fusion.5
  109.8 1.9 constant_dynamic-update-slice_fusion.4
  111.7 0.8 constant_dynamic-update-slice_fusion.3
  112.5 0.8 constant_dynamic-update-slice_fusion.2
  113.4 0.8 constant_dynamic-update-slice_fusion.1
  114.2 3.5 %collective-permute-done.14 = bf16[512,512]{1,0:T(8,128)(2,1)S(1)} collective-permute-done((bf16[512,512]{1,0:T(8,128)(2,1)S(1)}, bf16[512,512]{1,0:T(8,128)(2,1)S(1)}, u32[]{:S(2)}, u32[]{:S(2)}) %collective-permute-start.14) | collective-permute-done | bytes 524320 | tf_op jit(solution)/shard_map/ppermute | solution.py:21
  117.6 0.8 constant_dynamic-update-slice_fusion
  118.5 6.5 %fusion.27 = bf16[128,512]{0,1:T(8,128)(2,1)} fusion(f32[128,512]{0,1:T(8,128)S(1)} %convolution_multiply_fusion, bf16[8192,512]{1,0:T(8,128)(2,1)} %constant_dynamic-update-slice_fusion, bf16[128,8192]{1,0:T(8,128)(2,1)S(1)} %copy-done), kind=kOutput, calls=%fused_computation.37 | convolution fusion | flops 1073872896 | bytes 10878976 | tf_op jit(solution)/shard_map/dot_general | solution.py:45
  125.0 0.6 dynamic-slice
  126.3 0.2 dynamic-update-slice
  126.5 14.2 %all-reduce = s32[32]{0:T(128)S(1)} all-reduce(s32[32]{0:T(128)S(1)} %dynamic-update-slice), channel_id=1, replica_groups=mesh['group'=2,'ctx'=16] {'ctx'}, use_global_device_ids=true, to_apply=%add | all-reduce | flops 32 | bytes 256
  140.7 0.1 iota_add_fusion.1
  140.8 0.7 slice_reduce_fusion.1
  141.4 0.7 iota_add_fusion
  144.6 25.4 %all-gather.5.cloned.1.call-done = bf16[2048,512]{0,1:T(8,128)(2,1)} async-done(((bf16[128,512]{0,1:T(8,128)(2,1)}), bf16[2048,512]{0,1:T(8,128)(2,1)}) %all-gather.5.cloned.1.call-update) | async-done | bytes 2097168 | tf_op jit(solution)/shard_map/all_gather | solution.py:76
  170.0 13.6 %conditional.2 = (f32[4,8,64]{2,1,0:T(8,128)S(1)}, f32[4,8,64,128]{3,2,1,0:T(8,128)S(1)}) conditional(s32[]{:T(128)} %convert_element_type.36, () %tuple.21, (s32[1,64]{1,0:T(1,128)S(1)}, s32[32,64]{1,0:T(8,128)S(1)}, bf16[128,4096]{1,0:T(8,128)(2,1)S(1)}, bf16[2048,4,128]{0,2,1:T(8,128)(2,1)}, bf16[2048,4,128]{0,2,1:T(8,128)(2,1)}) %tuple.48), branch_computations={%region_2.3_spmd, %region_3.6_spmd} | conditional | flops 2202138624 | bytes 67182896 | solution.py:105
  170.0 0.1 ge.34
  170.0 0.1 broadcast_compare_fusion
  170.2 0.1 copy.36
  170.3 4.6 %fusion = (f32[4,8,64]{2,1,0:T(8,128)S(1)}, f32[4,2048,64,8]{1,2,3,0:T(8,128)S(1)}) fusion(pred[64,2048]{1,0:T(8,128)(4,1)S(1)} %broadcast_compare_fusion, bf16[64,4,8,128]{3,2,1,0:T(8,128)(2,1)S(1)} %bitcast.84, bf16[2048,4,128]{0,2,1:T(8,128)(2,1)} %get-tuple-element.62), kind=kOutput, calls=%fused_computation.2 | convolution fusion | flops 1086322688 | bytes 19537920 | tf_op jit(solution)/shard_map/cond/branch_1_fun/tkgd,skd->kgts/dot_general | solution.py:86
  174.9 3.5 %fusion.3 = f32[4,8,64,128]{3,2,1,0:T(8,128)S(1)} fusion(f32[4,2048,64,8]{1,2,3,0:T(8,128)S(1)} %get-tuple-element.72, f32[4,8,64]{2,1,0:T(8,128)S(1)} %broadcast_maximum_fusion, pred[64,2048]{1,0:T(8,128)(4,1)S(1)} %broadcast_compare_fusion, bf16[2048,4,128]{0,2,1:T(8,128)(2,1)S(1)} %copy-done.4), kind=kOutput, calls=%fused_computation.5 | convolution fusion | flops 1094713344 | bytes 20062208 | tf_op jit(solution)/shard_map/cond/branch_1_fun/kgts,skd->kgtd/dot_general | solution.py:94
  178.5 5.1 %fusion.2 = f32[4,8,64]{2,1,0:T(8,128)S(1)} fusion(f32[4,2048,64,8]{1,2,3,0:T(8,128)S(1)} %get-tuple-element.72, f32[4,8,64]{2,1,0:T(8,128)S(1)} %broadcast_maximum_fusion, pred[64,2048]{1,0:T(8,128)(4,1)S(1)} %broadcast_compare_fusion), kind=kLoop, calls=%fused_computation.4 | loop fusion | flops 20969472 | bytes 16924672 | tf_op jit(solution)/shard_map/cond/branch_1_fun/reduce_sum | solution.py:93
  183.6 0.3 fusion.28
  183.9 1.1 copy.19
  185.0 13.6 %conditional.3 = (f32[4,8,64]{2,1,0:T(8,128)S(1)}, f32[4,8,64,128]{3,2,1,0:T(8,128)S(1)}) conditional(s32[]{:T(128)} %convert_element_type.42, () %tuple.23, (s32[1,64]{1,0:T(1,128)S(1)}, s32[32,64]{1,0:T(8,128)S(1)}, bf16[128,4096]{1,0:T(8,128)(2,1)S(1)}, bf16[2048,4,128]{0,2,1:T(8,128)(2,1)}, bf16[2048,4,128]{0,2,1:T(8,128)(2,1)}) %tuple.49), branch_computations={%region_7.8_spmd, %region_8.11_spmd} | conditional | flops 2202138624 | bytes 67182896 | solution.py:105
  185.0 0.1 ge.39
  185.1 0.1 broadcast_compare_fusion.1
  185.3 0.1 copy.37
  185.4 4.6 %fusion.13 = (f32[4,8,64]{2,1,0:T(8,128)S(1)}, f32[4,2048,64,8]{1,2,3,0:T(8,128)S(1)}) fusion(pred[64,2048]{1,0:T(8,128)(4,1)S(1)} %broadcast_compare_fusion.1, bf16[64,4,8,128]{3,2,1,0:T(8,128)(2,1)S(1)} %bitcast.85, bf16[2048,4,128]{0,2,1:T(8,128)(2,1)} %get-tuple-element.67), kind=kOutput, calls=%fused_computation.19 | convolution fusion | flops 1086322688 | bytes 19537920 | tf_op jit(solution)/shard_map/cond/branch_1_fun/tkgd,skd->kgts/dot_general | solution.py:86
  190.0 3.5 %fusion.16 = f32[4,8,64,128]{3,2,1,0:T(8,128)S(1)} fusion(f32[4,2048,64,8]{1,2,3,0:T(8,128)S(1)} %get-tuple-element.74, f32[4,8,64]{2,1,0:T(8,128)S(1)} %broadcast_maximum_fusion.1, pred[64,2048]{1,0:T(8,128)(4,1)S(1)} %broadcast_compare_fusion.1, bf16[2048,4,128]{0,2,1:T(8,128)(2,1)S(1)} %copy-done.5), kind=kOutput, calls=%fused_computation.22 | convolution fusion | flops 1094713344 | bytes 20062208 | tf_op jit(solution)/shard_map/cond/branch_1_fun/kgts,skd->kgtd/dot_general | solution.py:94
  193.6 5.1 %fusion.15 = f32[4,8,64]{2,1,0:T(8,128)S(1)} fusion(f32[4,2048,64,8]{1,2,3,0:T(8,128)S(1)} %get-tuple-element.74, f32[4,8,64]{2,1,0:T(8,128)S(1)} %broadcast_maximum_fusion.1, pred[64,2048]{1,0:T(8,128)(4,1)S(1)} %broadcast_compare_fusion.1), kind=kLoop, calls=%fused_computation.21 | loop fusion | flops 20969472 | bytes 16924672 | tf_op jit(solution)/shard_map/cond/branch_1_fun/reduce_sum | solution.py:93
  198.6 0.3 fusion.29
  199.0 0.3 copy.22
  199.3 1.4 copy_bitcast_fusion
  200.8 1.1 pad_maximum_fusion
  (41 shorter events, 0.3 us)
Async XLA Ops:
  6.5 58.3 %copy-start = (bf16[128,8192]{1,0:T(8,128)(2,1)S(1)}, bf16[128,8192]{1,0:T(8,128)(2,1)}, u32[]{:S(2)}) copy-start(bf16[128,8192]{1,0:T(8,128)(2,1)} %param.11) | copy-start | bytes 6291460
  6.5 76.0 %copy-start.3 = (bf16[512,512]{1,0:T(8,128)(2,1)S(1)}, bf16[512,512]{1,0:T(8,128)(2,1)}, u32[]{:S(2)}) copy-start(bf16[512,512]{1,0:T(8,128)(2,1)} %param.14) | copy-start | bytes 1572868
  6.5 138.1 %all-gather.3.cloned.1.call-start = ((), (), s32[]{:S(2)}) async-start(), calls=%async_computation | async-start | bytes 2228224 | tf_op jit(solution)/shard_map/all_gather | solution.py:72
  6.5 12.8 %collective-permute-start = (bf16[512,512]{1,0:T(8,128)(2,1)}, bf16[512,512]{1,0:T(8,128)(2,1)}, u32[]{:S(2)}, u32[]{:S(2)}) collective-permute-start(bf16[512,512]{1,0:T(8,128)(2,1)} %param.14), channel_id=1, source_target_pairs={{0,1},{1,2},{2,3},{3,4},{4,5},{5,6},{6,7},{7,8},{8,9},{9,10},{10,1... | collective-permute-start | bytes 1572872 | tf_op jit(solution)/shard_map/ppermute | solution.py:21
  7.0 14.7 %collective-permute-start.1 = (bf16[512,512]{1,0:T(8,128)(2,1)}, bf16[512,512]{1,0:T(8,128)(2,1)}, u32[]{:S(2)}, u32[]{:S(2)}) collective-permute-start(bf16[512,512]{1,0:T(8,128)(2,1)} %param.14), channel_id=1, source_target_pairs={{0,15},{1,0},{2,1},{3,2},{4,3},{5,4},{6,5},{7,6},{8,7},{9,8},{10,9... | collective-permute-start | bytes 1572872 | tf_op jit(solution)/shard_map/ppermute | solution.py:24
  19.3 11.7 %collective-permute-start.2 = (bf16[512,512]{1,0:T(8,128)(2,1)}, bf16[512,512]{1,0:T(8,128)(2,1)}, u32[]{:S(2)}, u32[]{:S(2)}) collective-permute-start(bf16[512,512]{1,0:T(8,128)(2,1)} %collective-permute-done), channel_id=1, source_target_pairs={{0,1},{1,2},{2,3},{3,4},{4,5},{5,6},{6,7},{7,8},{8,9},{9,10},{10,1... | collective-permute-start | bytes 1572872 | tf_op jit(solution)/shard_map/ppermute | solution.py:21
  21.7 13.8 %collective-permute-start.3 = (bf16[512,512]{1,0:T(8,128)(2,1)}, bf16[512,512]{1,0:T(8,128)(2,1)}, u32[]{:S(2)}, u32[]{:S(2)}) collective-permute-start(bf16[512,512]{1,0:T(8,128)(2,1)} %collective-permute-done.1), channel_id=1, source_target_pairs={{0,15},{1,0},{2,1},{3,2},{4,3},{5,4},{6,5},{7,6},{8,7},{9,8},{10,9... | collective-permute-start | bytes 1572872 | tf_op jit(solution)/shard_map/ppermute | solution.py:24
  31.0 11.6 %collective-permute-start.4 = (bf16[512,512]{1,0:T(8,128)(2,1)}, bf16[512,512]{1,0:T(8,128)(2,1)S(1)}, u32[]{:S(2)}, u32[]{:S(2)}) collective-permute-start(bf16[512,512]{1,0:T(8,128)(2,1)} %collective-permute-done.2), channel_id=1, source_target_pairs={{0,1},{1,2},{2,3},{3,4},{4,5},{5,6},{6,7},{7,8},{8,9},{9,10},{10,1... | collective-permute-start | bytes 1572872 | tf_op jit(solution)/shard_map/ppermute | solution.py:21
  35.5 15.5 %collective-permute-start.5 = (bf16[512,512]{1,0:T(8,128)(2,1)}, bf16[512,512]{1,0:T(8,128)(2,1)}, u32[]{:S(2)}, u32[]{:S(2)}) collective-permute-start(bf16[512,512]{1,0:T(8,128)(2,1)} %collective-permute-done.3), channel_id=1, source_target_pairs={{0,15},{1,0},{2,1},{3,2},{4,3},{5,4},{6,5},{7,6},{8,7},{9,8},{10,9... | collective-permute-start | bytes 1572872 | tf_op jit(solution)/shard_map/ppermute | solution.py:24
  42.7 11.4 %collective-permute-start.6 = (bf16[512,512]{1,0:T(8,128)(2,1)S(1)}, bf16[512,512]{1,0:T(8,128)(2,1)}, u32[]{:S(2)}, u32[]{:S(2)}) collective-permute-start(bf16[512,512]{1,0:T(8,128)(2,1)S(1)} %collective-permute-done.4), channel_id=1, source_target_pairs={{0,1},{1,2},{2,3},{3,4},{4,5},{5,6},{6,7},{7,8},{8,9},{9,10},{10,1... | collective-permute-start | bytes 1572872 | tf_op jit(solution)/shard_map/ppermute | solution.py:21
  50.9 119.0 %all-gather.5.cloned.1.call-start = ((), (), s32[]{:S(2)}) async-start(), calls=%async_computation.1 | async-start | bytes 2228224 | tf_op jit(solution)/shard_map/all_gather | solution.py:76
  51.0 13.8 %collective-permute-start.7 = (bf16[512,512]{1,0:T(8,128)(2,1)}, bf16[512,512]{1,0:T(8,128)(2,1)}, u32[]{:S(2)}, u32[]{:S(2)}) collective-permute-start(bf16[512,512]{1,0:T(8,128)(2,1)} %collective-permute-done.5), channel_id=1, source_target_pairs={{0,15},{1,0},{2,1},{3,2},{4,3},{5,4},{6,5},{7,6},{8,7},{9,8},{10,9... | collective-permute-start | bytes 1572872 | tf_op jit(solution)/shard_map/ppermute | solution.py:24
  54.1 12.9 %collective-permute-start.8 = (bf16[512,512]{1,0:T(8,128)(2,1)}, bf16[512,512]{1,0:T(8,128)(2,1)}, u32[]{:S(2)}, u32[]{:S(2)}) collective-permute-start(bf16[512,512]{1,0:T(8,128)(2,1)} %collective-permute-done.6), channel_id=1, source_target_pairs={{0,1},{1,2},{2,3},{3,4},{4,5},{5,6},{6,7},{7,8},{8,9},{9,10},{10,1... | collective-permute-start | bytes 1572872 | tf_op jit(solution)/shard_map/ppermute | solution.py:21
  64.8 24.3 %collective-permute-start.9 = (bf16[512,512]{1,0:T(8,128)(2,1)}, bf16[512,512]{1,0:T(8,128)(2,1)}, u32[]{:S(2)}, u32[]{:S(2)}) collective-permute-start(bf16[512,512]{1,0:T(8,128)(2,1)} %collective-permute-done.7), channel_id=1, source_target_pairs={{0,15},{1,0},{2,1},{3,2},{4,3},{5,4},{6,5},{7,6},{8,7},{9,8},{10,9... | collective-permute-start | bytes 1572872 | tf_op jit(solution)/shard_map/ppermute | solution.py:24
  67.0 24.0 %collective-permute-start.10 = (bf16[512,512]{1,0:T(8,128)(2,1)}, bf16[512,512]{1,0:T(8,128)(2,1)}, u32[]{:S(2)}, u32[]{:S(2)}) collective-permute-start(bf16[512,512]{1,0:T(8,128)(2,1)} %collective-permute-done.8), channel_id=1, source_target_pairs={{0,1},{1,2},{2,3},{3,4},{4,5},{5,6},{6,7},{7,8},{8,9},{9,10},{10,1... | collective-permute-start | bytes 1572872 | tf_op jit(solution)/shard_map/ppermute | solution.py:21
  89.0 11.4 %collective-permute-start.11 = (bf16[512,512]{1,0:T(8,128)(2,1)}, bf16[512,512]{1,0:T(8,128)(2,1)S(1)}, u32[]{:S(2)}, u32[]{:S(2)}) collective-permute-start(bf16[512,512]{1,0:T(8,128)(2,1)} %collective-permute-done.9), channel_id=1, source_target_pairs={{0,15},{1,0},{2,1},{3,2},{4,3},{5,4},{6,5},{7,6},{8,7},{9,8},{10,9... | collective-permute-start | bytes 1572872 | tf_op jit(solution)/shard_map/ppermute | solution.py:24
  91.0 14.3 %collective-permute-start.12 = (bf16[512,512]{1,0:T(8,128)(2,1)}, bf16[512,512]{1,0:T(8,128)(2,1)S(1)}, u32[]{:S(2)}, u32[]{:S(2)}) collective-permute-start(bf16[512,512]{1,0:T(8,128)(2,1)} %collective-permute-done.10), channel_id=1, source_target_pairs={{0,1},{1,2},{2,3},{3,4},{4,5},{5,6},{6,7},{7,8},{8,9},{9,10},{10,1... | collective-permute-start | bytes 1572872 | tf_op jit(solution)/shard_map/ppermute | solution.py:21
  100.4 12.9 %collective-permute-start.13 = (bf16[512,512]{1,0:T(8,128)(2,1)S(1)}, bf16[512,512]{1,0:T(8,128)(2,1)S(1)}, u32[]{:S(2)}, u32[]{:S(2)}) collective-permute-start(bf16[512,512]{1,0:T(8,128)(2,1)S(1)} %collective-permute-done.11), channel_id=1, source_target_pairs={{0,15},{1,0},{2,1},{3,2},{4,3},{5,4},{6,5},{7,6},{8,7},{9,8},{10,9... | collective-permute-start | bytes 1572872 | tf_op jit(solution)/shard_map/ppermute | solution.py:24
  105.3 12.4 %collective-permute-start.14 = (bf16[512,512]{1,0:T(8,128)(2,1)S(1)}, bf16[512,512]{1,0:T(8,128)(2,1)S(1)}, u32[]{:S(2)}, u32[]{:S(2)}) collective-permute-start(bf16[512,512]{1,0:T(8,128)(2,1)S(1)} %collective-permute-done.12), channel_id=1, source_target_pairs={{0,1},{1,2},{2,3},{3,4},{4,5},{5,6},{6,7},{7,8},{8,9},{9,10},{10,1... | collective-permute-start | bytes 1572872 | tf_op jit(solution)/shard_map/ppermute | solution.py:21
  118.5 6.6 %copy-start.7 = (u32[32]{0:T(128)S(1)}, u32[32]{0:T(128)}, u32[]{:S(2)}) copy-start(u32[32]{0:T(128)} %constant.147) | copy-start | bytes 388
  118.5 7.8 %copy-start.6 = (s32[2]{0:T(128)S(1)}, s32[2]{0:T(128)}, u32[]{:S(2)}) copy-start(s32[2]{0:T(128)} %param.17) | copy-start | bytes 28
  118.5 51.5 %copy-start.2 = (bf16[128,4096]{1,0:T(8,128)(2,1)S(1)}, bf16[128,4096]{1,0:T(8,128)(2,1)}, u32[]{:S(2)}) copy-start(bf16[128,4096]{1,0:T(8,128)(2,1)} %param.12) | copy-start | bytes 3145732
  170.3 4.6 %copy-start.4 = (bf16[2048,4,128]{0,2,1:T(8,128)(2,1)S(1)}, bf16[2048,4,128]{0,2,1:T(8,128)(2,1)}, u32[]{:S(2)}) copy-start(bf16[2048,4,128]{0,2,1:T(8,128)(2,1)} %get-tuple-element.63) | copy-start | bytes 6291460 | tf_op jit(solution)/shard_map/cond
  185.4 4.6 %copy-start.5 = (bf16[2048,4,128]{0,2,1:T(8,128)(2,1)S(1)}, bf16[2048,4,128]{0,2,1:T(8,128)(2,1)}, u32[]{:S(2)}) copy-start(bf16[2048,4,128]{0,2,1:T(8,128)(2,1)} %get-tuple-element.68) | copy-start | bytes 6291460 | tf_op jit(solution)/shard_map/cond
  198.6 3.2 %copy-start.1 = (bf16[128,8192]{1,0:T(8,128)(2,1)S(1)}, bf16[128,8192]{1,0:T(8,128)(2,1)}, u32[]{:S(2)}) copy-start(bf16[128,8192]{1,0:T(8,128)(2,1)} %param.11) | copy-start | bytes 6291460
Sparse Core Ops, SparseCore 0:
  51.1 50.1 all-gather.2
  125.1 44.7 all-gather.4
